TPU v7x, 32 devices: a whole 2x2x4 slice. The times are simulated.
32 devices in a mesh: group: 2 (over y), tensor: 4 (over z), dp: 4 (over x, core).
Axes of the slice: x: 2, y: 2, z: 4, core: 2. Of those that a mesh axis runs over, the one named last changes fastest.
Arguments:
- teacher_input: bfloat16 [16, 257, 6144], P(('group', 'dp')), parts along dimension 0, may hold values from -1000 to 1000
- teacher_gain: float32 [6144], replicated, may hold values from 0.5 to 2
- teacher_weight: bfloat16 [6144, 2, 6144], P('dp', None, 'tensor'), may hold values from -30 to 30
- head_counts: int32 [48, 16], replicated, may hold values from 0 to 3
- assignment: int32 [16], P(('group', 'dp')), parts along dimension 0, may hold values from 0 to 7, each once
- student_input: bfloat16 [16, 257, 1024], P(('group', 'dp')), parts along dimension 0, may hold values from -1000 to 1000
- student_gain: float32 [1024], replicated, may hold values from 0.5 to 2
- student_bias: float32 [1024], replicated, may hold values from -3 to 3
- student_weight: bfloat16 [1024, 2048], P(None, 'tensor'), may hold values from -30 to 30
Outputs:
- weight_grad: float32 [2048, 2048], P('group', 'tensor'), parts along dimension 0
There are 2 independent parts, one for each index of `group`. A program takes and returns all parts, laid end to end along the dimension named above; an argument that names none is the same for every part. Nothing has to cross between parts.
Inputs may be any that keep to these rules, and one draw needn't show every extreme that they name: `assignment`: every image index of the group appears exactly once.
All inputs are finite; a program needn't handle non-finite values.
Results may differ from a plain program's by a relative error of at most 0.013.
The roundings to bfloat16 on the way count: a program that leaves them out, or rounds other values in their place, can miss the bound.
Values may be sent and summed in bfloat16 or wider, within the bound.
A program may use at most 192 MiB of HBM per device.

v0:
```python
import jax
import jax.numpy as jnp
from jax import lax
from jax.sharding import PartitionSpec as P

HD_T = 128
D_S = 1024
HD_S = 64
QROWS = 128
DIVISOR = 72


def layer_norm(values, gain, shift):
    wide = values.astype(jnp.float32)
    center = wide - jnp.mean(wide, axis=-1, keepdims=True)
    spread = jnp.mean(center * center, axis=-1, keepdims=True)
    return center * lax.rsqrt(spread + 1e-06) * gain + shift


def on_device(
    teacher_input,
    teacher_gain,
    teacher_weight,
    head_counts,
    assignment,
    student_input,
    student_gain,
    student_bias,
    student_weight,
):
    images = teacher_input.shape[0]
    tokens = teacher_input.shape[1]
    width_t = teacher_input.shape[2]
    teacher_cols = teacher_weight.shape[2]
    heads_here = teacher_cols // HD_T
    student_heads = student_weight.shape[1] // (2 * HD_S)
    tensor_place = lax.axis_index("tensor")
    teacher_normed = layer_norm(teacher_input, teacher_gain, 0.0).astype(jnp.bfloat16)
    normed_query = teacher_normed[:, :QROWS].reshape(images * QROWS, width_t)
    normed_keys = teacher_normed.reshape(images * tokens, width_t)
    piece = lax.all_gather(teacher_weight, "dp", axis=0, tiled=True)
    new_query = jnp.dot(normed_query, piece[:, 0, :], preferred_element_type=jnp.float32)
    new_keys = jnp.dot(normed_keys, piece[:, 1, :], preferred_element_type=jnp.float32)
    teacher_query = (
        (new_query * HD_T ** (-0.5)).astype(jnp.bfloat16).reshape(images, QROWS, heads_here, HD_T)
    )
    teacher_keys = new_keys.astype(jnp.bfloat16).reshape(images, tokens, heads_here, HD_T)
    teacher_scores = jnp.einsum(
        "bqhd,bkhd->bhqk", teacher_query, teacher_keys, preferred_element_type=jnp.float32
    )
    teacher_maps = jax.nn.softmax(teacher_scores, axis=-1).astype(jnp.bfloat16)
    own_counts = lax.dynamic_slice_in_dim(
        head_counts, tensor_place * heads_here, heads_here, 0
    ).astype(jnp.bfloat16)
    folded = lax.psum_scatter(
        (
            jnp.einsum(
                "bgqk,gs->sbqk", teacher_maps, own_counts, preferred_element_type=jnp.float32
            )
            / DIVISOR
        ).astype(jnp.bfloat16),
        "tensor",
        scatter_dimension=0,
        tiled=True,
    )
    piece = lax.all_gather(folded, "dp", axis=1, tiled=True)
    width_piece = piece.shape[1]
    positions = jnp.arange(width_piece, dtype=jnp.int32)
    picker = (assignment[:, None] == positions[None, :]).astype(jnp.bfloat16)
    target = jnp.einsum("ji,hiqk->hjqk", picker, piece, preferred_element_type=jnp.float32).astype(
        jnp.bfloat16
    )
    student_normed = layer_norm(student_input, student_gain, student_bias).astype(jnp.bfloat16)
    normed_front = student_normed[:, :QROWS]
    packed = student_weight.reshape(D_S, student_heads, 2, HD_S)
    weight_query = packed[:, :, 0, :].reshape(D_S, student_heads * HD_S)
    weight_key = packed[:, :, 1, :].reshape(D_S, student_heads * HD_S)
    student_query = (
        jnp.einsum("btd,dc->btc", normed_front, weight_query, preferred_element_type=jnp.float32)
        * HD_S ** (-0.5)
    ).astype(jnp.bfloat16)
    student_keys = jnp.einsum(
        "btd,dc->btc", student_normed, weight_key, preferred_element_type=jnp.float32
    ).astype(jnp.bfloat16)
    split_query = student_query.reshape(images, QROWS, student_heads, HD_S)
    split_keys = student_keys.reshape(images, tokens, student_heads, HD_S)
    probs = jax.nn.softmax(
        jnp.einsum("bqhd,bkhd->hbqk", split_query, split_keys, preferred_element_type=jnp.float32),
        axis=-1,
    )
    target_wide = target.astype(jnp.float32)
    score_grad = (probs * jnp.sum(target_wide, axis=-1, keepdims=True) - target_wide).astype(
        jnp.bfloat16
    )
    query_grad = (
        jnp.einsum("hbqk,bkhd->bqhd", score_grad, split_keys, preferred_element_type=jnp.float32)
        * HD_S ** (-0.5)
    ).astype(jnp.bfloat16)
    key_grad = jnp.einsum(
        "hbqk,bqhd->bkhd", score_grad, split_query, preferred_element_type=jnp.float32
    ).astype(jnp.bfloat16)
    grad_query = jnp.einsum(
        "fkm,fkp->mp",
        normed_front,
        query_grad.reshape(images, QROWS, student_heads * HD_S),
        preferred_element_type=jnp.float32,
    )
    grad_key = jnp.einsum(
        "oip,ois->ps",
        student_normed,
        key_grad.reshape(images, tokens, student_heads * HD_S),
        preferred_element_type=jnp.float32,
    )
    local_grad = jnp.stack(
        [grad_query.reshape(D_S, student_heads, HD_S), grad_key.reshape(D_S, student_heads, HD_S)],
        axis=2,
    )
    local_grad = local_grad.reshape(D_S, student_heads * 2 * HD_S)
    return lax.psum(local_grad.astype(jnp.bfloat16), "dp").astype(jnp.float32)


def solution(mesh):
    placed = (
        P(("group", "dp"), None, None),
        P(),
        P("dp", None, "tensor"),
        P(),
        P(("group", "dp")),
        P(("group", "dp"), None, None),
        P(),
        P(),
        P(None, "tensor"),
    )
    return jax.shard_map(
        on_device, mesh=mesh, in_specs=placed, out_specs=P("group", "tensor"), check_vma=False
    )
```

profile of v0, /device:TPU:0, one launch (start us, length us, event | category | flops | bytes accessed | tf_op | source)
XLA Modules:
  0.0 448.8 jit_solution(8952922629155033750)
XLA Ops:
  6.5 8.8 %copy.104 = bf16[1536,2,1536]{2,0,1:T(8,128)(2,1)} copy(bf16[1536,2,1536]{2,1,0:T(2,128)(2,1)} %param.11) | data formatting | bytes 18874368 | tf_op args[2]
  15.4 6.3 %convert_reduce_fusion = f32[2,257]{1,0:T(2,128)S(1)} fusion(bf16[2,257,6144]{2,0,1:T(2,128)(2,1)} %param.9), kind=kLoop, calls=%fused_computation.6 | loop fusion | flops 6315518 | bytes 6318088 | tf_op jit(solution)/shard_map/reduce_sum | solution.py:15
  21.7 3.5 fusion.5
  25.2 4.1 fusion.7
  29.4 4.6 %copy-done.1 = bf16[2,257,6144]{2,1,0:T(8,128)(2,1)} copy-done((bf16[2,257,6144]{2,1,0:T(8,128)(2,1)}, bf16[2,257,6144]{2,1,0:T(8,128)(2,1)S(1)}, u32[]{:S(2)}) %copy-start.1) | copy-done | bytes 6316056
  34.0 9.8 %reshape.81 = bf16[514,6144]{1,0:T(8,128)(2,1)} reshape(bf16[2,257,6144]{2,1,0:T(8,128)(2,1)} %copy-done.1) | data formatting | bytes 12632064 | tf_op jit(solution)/shard_map/reshape | solution.py:40
  43.7 202.4 %all-gather.3.cloned.1.call-done = bf16[6144,2,1536]{2,0,1:T(8,128)(2,1)} async-done(((bf16[1536,2,1536]{2,0,1:T(8,128)(2,1)}), bf16[6144,2,1536]{2,0,1:T(8,128)(2,1)}) %all-gather.3.cloned.1.call-update) | async-done | bytes 37748752 | tf_op jit(solution)/shard_map/all_gather | solution.py:41
  246.1 10.2 %fusion.10 = bf16[256,1536]{1,0:T(8,128)(2,1)} fusion(bf16[256,6144]{1,0:T(8,128)(2,1)S(1)} %bitcast.99, bf16[6144,2,1536]{2,0,1:T(8,128)(2,1)} %all-gather.3.cloned.1.call-done), kind=kOutput, calls=%fused_computation.19 | convolution fusion | flops 4832624640 | bytes 22806528 | tf_op jit(solution)/shard_map/dot_general | solution.py:42
  256.3 2.4 reshape.95
  258.6 16.2 %fusion.8 = bf16[514,1536]{1,0:T(8,128)(2,1)S(1)} fusion(bf16[514,6144]{1,0:T(8,128)(2,1)} %reshape.81, bf16[6144,2,1536]{2,0,1:T(8,128)(2,1)} %all-gather.3.cloned.1.call-done), kind=kOutput, calls=%fused_computation.15 | convolution fusion | flops 9702214656 | bytes 26843136 | tf_op jit(solution)/shard_map/dot_general | solution.py:43
  274.8 2.4 reshape.82
  277.2 3.1 fusion.61
  281.1 0.8 multiply_convert_fusion
  281.8 2.9 copy.109
  284.9 0.6 dynamic-slice
  286.1 85.7 %all-reduce.6.cloned.1.call-done = bf16[16,2,128,257]{2,1,3,0:T(2,128)(2,1)} async-done(((bf16[16,2,128,257]{2,1,3,0:T(2,128)(2,1)}), bf16[16,2,128,257]{2,1,3,0:T(2,128)(2,1)}) %all-reduce.6.cloned.1.call-update) | async-done | bytes 2105360
  371.8 1.4 constant_dynamic-slice_fusion
  373.2 1.0 copy.110
  374.3 0.8 copy.94
  376.1 0.8 convolution_convert_fusion.1
  377.1 0.5 fusion.16
  377.6 1.0 copy-done.3
  379.0 0.5 fusion.66
  379.6 0.5 fusion.34
  380.1 16.0 %all-gather.5.cloned.1.call-done = bf16[4,8,128,257]{2,0,3,1:T(4,128)(2,1)} async-done(((bf16[4,2,128,257]{2,0,3,1:T(4,128)(2,1)}), bf16[4,8,128,257]{2,0,3,1:T(4,128)(2,1)}) %all-gather.5.cloned.1.call-update) | async-done | bytes 2105360 | tf_op jit(solution)/shard_map/all_gather | solution.py:66
  396.1 2.4 fusion.17
  398.8 0.7 fusion.31
  399.4 1.5 fusion.24
  401.0 1.0 fusion.25
  402.1 1.1 copy.117
  403.2 36.5 %all-reduce.4.cloned.1.call-done = bf16[1024,512]{0,1:T(8,128)(2,1)} async-done(((bf16[1024,512]{0,1:T(8,128)(2,1)}), bf16[1024,512]{0,1:T(8,128)(2,1)}) %all-reduce.4.cloned.1.call-update) | async-done | bytes 1048592 | tf_op jit(solution)/shard_map/psum | solution.py:119
  439.7 2.6 copy.118
  (44 shorter events, 3.0 us)
Async XLA Ops:
  6.5 239.5 %all-gather.3.cloned.1.call-start = ((), (), s32[]{:S(2)}) async-start(), calls=%async_computation | async-start | bytes 47185920 | tf_op jit(solution)/shard_map/all_gather | solution.py:41
  15.3 356.5 %all-reduce.6.cloned.1.call-start = ((), (), s32[]{:S(2)}) async-start(), calls=%async_computation.3 | async-start | bytes 4210688
  15.4 6.3 %copy-start = (bf16[2,257,6144]{2,0,1:T(2,128)(2,1)S(1)}, bf16[2,257,6144]{2,0,1:T(2,128)(2,1)}, u32[]{:S(2)}) copy-start(bf16[2,257,6144]{2,0,1:T(2,128)(2,1)} %param.9) | copy-start | bytes 18948100
  21.7 3.5 copy-start.5
  29.4 4.6 %copy-start.1 = (bf16[2,257,6144]{2,1,0:T(8,128)(2,1)}, bf16[2,257,6144]{2,1,0:T(8,128)(2,1)S(1)}, u32[]{:S(2)}) copy-start(bf16[2,257,6144]{2,1,0:T(8,128)(2,1)S(1)} %fusion.7) | copy-start | bytes 18948100
  34.0 212.1 %slice-start = ((bf16[2,257,6144]{2,1,0:T(8,128)(2,1)}), bf16[2,128,6144]{2,1,0:T(8,128)(2,1)S(1)}, s32[]{:S(2)}) async-start(bf16[2,257,6144]{2,1,0:T(8,128)(2,1)} %copy-done.1), calls=%async_computation.4 | async-start | bytes 6291456 | tf_op jit(solution)/shard_map/slice | solution.py:39
  280.4 0.7 copy-start.6
  281.8 3.0 copy-start.10
  284.8 89.5 %copy-start.4 = (bf16[1024,512]{1,0:T(8,128)(2,1)S(1)}, bf16[1024,512]{1,0:T(8,128)(2,1)}, u32[]{:S(2)}) copy-start(bf16[1024,512]{1,0:T(8,128)(2,1)} %param.17) | copy-start | bytes 3145732
  284.8 111.3 %all-gather.5.cloned.1.call-start = ((), (), s32[]{:S(2)}) async-start(), calls=%async_computation.1 | async-start | bytes 2631680 | tf_op jit(solution)/shard_map/all_gather | solution.py:66
  286.1 89.0 %copy-start.2 = (bf16[2,257,1024]{2,0,1:T(2,128)(2,1)S(1)}, bf16[2,257,1024]{2,0,1:T(2,128)(2,1)}, u32[]{:S(2)}) copy-start(bf16[2,257,1024]{2,0,1:T(2,128)(2,1)} %param.14) | copy-start | bytes 3158020
  374.3 65.4 %all-reduce.4.cloned.1.call-start = ((), (), s32[]{:S(2)}) async-start(), calls=%async_computation.2 | async-start | bytes 2097152 | tf_op jit(solution)/shard_map/psum | solution.py:119
  375.1 0.9 copy-start.7
  375.1 0.9 copy-start.8
  377.6 1.0 copy-start.3
  378.6 17.5 %copy-start.9 = (s32[2]{0:T(128)S(1)}, s32[2]{0:T(128)}, u32[]{:S(2)}) copy-start(s32[2]{0:T(128)} %param.13) | copy-start | bytes 28
Sparse Core Ops, SparseCore 0:
  15.5 230.5 all-gather.2
  284.9 86.8 all-reduce.5
  374.4 21.6 all-gather.4
  403.3 36.2 all-reduce.3
where the time goes:
time: 449 us
  waiting for transfers between devices  341 us (76%)
  local copies, waits for them, and re-layouts  40.2 us (9%)
  matrix products  36.8 us (8%)
  other arithmetic  17.1 us (4%)
  between operations  14 us (3%)
    all_gather x1, waiting for transfers between devices, on_device(): piece = lax.all_gather(teacher_weight, 'dp', axis=0, tiled=True)  202 us
    unnamed x5, waiting for transfers between devices  85.8 us
    psum x1, waiting for transfers between devices, on_device(): return lax.psum(local_grad.astype(jnp.bfloat16), 'dp').astype(jnp.float32)  36.5 us
    unnamed x26, local copies, waits for them, and re-layouts  17.6 us
    dot_general x1, matrix products, on_device(): jnp.dot(normed_keys, piece[:, 1, :], preferred_element_type=jnp.float32)  16.2 us
    all_gather x1, waiting for transfers between devices, on_device(): piece = lax.all_gather(folded, 'dp', axis=1, tiled=True)  16 us
    dot_general x1, matrix products, on_device(): jnp.dot(normed_query, piece[:, 0, :], preferred_element_type=jnp.float32)  10.2 us
    reshape x1, local copies, waits for them, and re-layouts, on_device(): normed_keys = teacher_normed.reshape(images * tokens, width_t)  9.77 us
  transfers between devices with their start and end apart: 4, of which 4 were waited for; matrix products, arithmetic and copies ran while one was open for 6% of the time, Pallas kernels for 0%

commit v1 on v0

v1 whole, which is shorter than its diff:
```python
import functools

import jax
import jax.numpy as jnp
from jax import lax
from jax.experimental import pallas as pl
from jax.experimental.pallas import tpu as pltpu
from jax.sharding import PartitionSpec as P

HD_T = 128
HD_S = 64
QROWS = 128
DIVISOR = 72
CORES = 2
MESH = pl.DeviceIdType.MESH


def layer_norm(values, gain, shift):
    wide = values.astype(jnp.float32)
    center = wide - jnp.mean(wide, axis=-1, keepdims=True)
    spread = jnp.mean(center * center, axis=-1, keepdims=True)
    return center * lax.rsqrt(spread + 1e-06) * gain + shift


def rounded_up(value, unit):
    return -(-value // unit) * unit


def teacher_kernel(
    sizes,
    counts_ref,
    x_ref,
    gain_ref,
    w_ref,
    out_ref,
    wbuf,
    normed,
    acc,
    part,
    landed,
    own_sem,
    sx,
    rx,
    sy,
    ry,
    so,
    ro,
    spx,
    rpx,
    spy,
    rpy,
    sz,
    rz,
):
    n_dp, n_group, n_tensor, heads_here, s_heads, images, tokens = sizes
    n_x = n_dp // CORES
    rows = w_ref.shape[1]
    rows_part = rows // n_group
    pad = normed.shape[0] // images
    s_here = s_heads // n_tensor

    dp = lax.axis_index("dp")
    y = lax.axis_index("group")
    t = lax.axis_index("tensor")
    x = dp // CORES
    core = lax.rem(dp, CORES)
    mate = x * CORES + (1 - core)

    def x_peer(s):
        return lax.rem(x + s, n_x) * CORES + core

    def x_source(s):
        return lax.rem(x + n_x - s, n_x) * CORES + core

    barrier = pltpu.get_barrier_semaphore()
    waits = 0
    for s in range(1, n_x):
        pl.semaphore_signal(barrier, inc=1, device_id={"dp": x_peer(s)}, device_id_type=MESH)
        waits += 1
    pl.semaphore_signal(barrier, inc=1, device_id={"dp": mate}, device_id_type=MESH)
    waits += 1
    for s in range(1, n_group):
        pl.semaphore_signal(
            barrier, inc=1, device_id={"group": lax.rem(y + s, n_group)}, device_id_type=MESH
        )
        waits += 1
    for s in range(1, n_tensor):
        pl.semaphore_signal(
            barrier, inc=1, device_id={"tensor": lax.rem(t + s, n_tensor)}, device_id_type=MESH
        )
        waits += 1
    pl.semaphore_wait(barrier, waits)

    def cols(k):
        return pl.ds(pl.multiple_of(k * HD_T, HD_T), HD_T)

    def band(g):
        return pl.ds(pl.multiple_of(g * rows_part, 16), rows_part)

    def copy_x(k, s):
        return pltpu.make_async_remote_copy(
            src_ref=w_ref.at[:, band(y), cols(k)],
            dst_ref=wbuf.at[dp, :, band(y), cols(k)],
            send_sem=sx.at[k, s - 1],
            recv_sem=rx.at[k, s - 1],
            device_id={"dp": x_peer(s)},
            device_id_type=MESH,
        )

    def copy_own(k):
        return pltpu.make_async_remote_copy(
            src_ref=w_ref.at[:, :, cols(k)],
            dst_ref=wbuf.at[dp, :, :, cols(k)],
            send_sem=so.at[k],
            recv_sem=ro.at[k],
            device_id={"dp": mate},
            device_id_type=MESH,
        )

    def copy_y(k, s, g):
        where = (x_source(s), slice(None), band(y), cols(k))
        return pltpu.make_async_remote_copy(
            src_ref=wbuf.at[where],
            dst_ref=wbuf.at[where],
            send_sem=sy.at[k, s - 1, g - 1],
            recv_sem=ry.at[k, s - 1, g - 1],
            device_id={"group": lax.rem(y + g, n_group)},
            device_id_type=MESH,
        )

    def copy_mate_x(k, s):
        where = (x_source(s), slice(None), band(y), cols(k))
        return pltpu.make_async_remote_copy(
            src_ref=wbuf.at[where],
            dst_ref=wbuf.at[where],
            send_sem=spx.at[k, s - 1],
            recv_sem=rpx.at[k, s - 1],
            device_id={"dp": mate},
            device_id_type=MESH,
        )

    def copy_mate_y(k, s, g):
        where = (x_source(s), slice(None), band(lax.rem(y + n_group - g, n_group)), cols(k))
        return pltpu.make_async_remote_copy(
            src_ref=wbuf.at[where],
            dst_ref=wbuf.at[where],
            send_sem=spy.at[k, s - 1, g - 1],
            recv_sem=rpy.at[k, s - 1, g - 1],
            device_id={"dp": mate},
            device_id_type=MESH,
        )

    def open_sends(k, carry):
        for s in range(1, n_x):
            copy_x(k, s).start()
        copy_own(k).start()
        return carry

    lax.fori_loop(0, heads_here, open_sends, 0)
    own_copy = pltpu.make_async_copy(w_ref, wbuf.at[dp], own_sem)
    own_copy.start()

    gain = gain_ref[...]
    for i in range(images):

        def norm_rows(r, carry):
            block = layer_norm(x_ref[i, pl.ds(pl.multiple_of(r * 16, 16), 16), :], gain, 0.0)
            normed[pl.ds(pl.multiple_of(i * pad + r * 16, 16), 16), :] = block.astype(jnp.bfloat16)
            return carry

        whole = tokens // 16
        lax.fori_loop(0, whole, norm_rows, 0)
        rest = tokens - whole * 16
        if rest:
            last = layer_norm(x_ref[i, whole * 16 : tokens, :], gain, 0.0)
            normed[i * pad + whole * 16 : (i + 1) * pad, :] = jnp.concatenate(
                [last, jnp.zeros((16 - rest, last.shape[1]), jnp.float32)], axis=0
            ).astype(jnp.bfloat16)
    acc[...] = jnp.zeros_like(acc)
    own_copy.wait()

    def attend(k):
        keys = jnp.zeros((images * pad, HD_T), jnp.float32)
        query = jnp.zeros((images * QROWS, HD_T), jnp.float32)
        for d in range(n_dp):
            deep = slice(d * rows, (d + 1) * rows)
            keys += jnp.dot(
                normed[:, deep], wbuf[d, 1, :, cols(k)], preferred_element_type=jnp.float32
            )
            front = jnp.concatenate(
                [normed[i * pad : i * pad + QROWS, deep] for i in range(images)], axis=0
            )
            query += jnp.dot(front, wbuf[d, 0, :, cols(k)], preferred_element_type=jnp.float32)
        query = (query * HD_T ** (-0.5)).astype(jnp.bfloat16)
        keys = keys.astype(jnp.bfloat16)
        for i in range(images):
            scores = lax.dot_general(
                keys[i * pad : (i + 1) * pad],
                query[i * QROWS : (i + 1) * QROWS],
                (((1,), (1,)), ((), ())),
                preferred_element_type=jnp.float32,
            )
            spot = lax.broadcasted_iota(jnp.int32, scores.shape, 0)
            scores = jnp.where(spot < tokens, scores, -jnp.inf)
            power = jnp.exp(scores - jnp.max(scores, axis=0, keepdims=True))
            maps = power / jnp.sum(power, axis=0, keepdims=True)
            maps = maps.astype(jnp.bfloat16).astype(jnp.float32)
            for s in range(s_heads):
                count = counts_ref[t * heads_here + k, s].astype(jnp.float32)
                acc[s, i] += count * maps

    def step(k, carry):
        @pl.when(k < heads_here)
        def _():
            for s in range(1, n_x):
                copy_x(k, s).wait_recv()
                for g in range(1, n_group):
                    copy_y(k, s, g).start()
                copy_mate_x(k, s).start()

        @pl.when(k > 0)
        def _():
            j = k - 1
            for s in range(1, n_x):
                for g in range(1, n_group):
                    copy_y(j, s, g).wait_recv()
                    copy_mate_y(j, s, g).start()
            copy_own(j).wait_recv()
            for s in range(1, n_x):
                copy_mate_x(j, s).wait_recv()
                for g in range(1, n_group):
                    copy_mate_y(j, s, g).wait_recv()
            attend(j)

        return carry

    lax.fori_loop(0, heads_here + 1, step, 0)

    def copy_z(s):
        to = lax.rem(t + s, n_tensor)
        return pltpu.make_async_remote_copy(
            src_ref=part.at[pl.ds(to * s_here, s_here)],
            dst_ref=landed.at[s - 1],
            send_sem=sz.at[s - 1],
            recv_sem=rz.at[s - 1],
            device_id={"tensor": to},
            device_id_type=MESH,
        )

    part[...] = (acc[...] / DIVISOR).astype(jnp.bfloat16)
    for s in range(n_tensor - 1, 0, -1):
        copy_z(s).start()

    def drain(k, carry):
        for s in range(1, n_x):
            copy_x(k, s).wait_send()
            copy_mate_x(k, s).wait_send()
            for g in range(1, n_group):
                copy_y(k, s, g).wait_send()
                copy_mate_y(k, s, g).wait_send()
        copy_own(k).wait_send()
        return carry

    lax.fori_loop(0, heads_here, drain, 0)
    for s in range(1, n_tensor):
        copy_z(s).wait()
    for h in range(s_here):
        total = part[t * s_here + h].astype(jnp.float32)
        for s in range(1, n_tensor):
            total += landed[s - 1, h].astype(jnp.float32)
        out_ref[h] = total.astype(jnp.bfloat16)


def teacher_folded(mesh_sizes, teacher_input, teacher_gain, teacher_weight, head_counts):
    n_dp, n_group, n_tensor = mesh_sizes
    images, tokens, width = teacher_input.shape
    rows, _, width_here = teacher_weight.shape
    heads_here = width_here // HD_T
    s_heads = head_counts.shape[1]
    s_here = s_heads // n_tensor
    pad = rounded_up(tokens, 16)
    n_x = n_dp // CORES
    split = jnp.transpose(teacher_weight, (1, 0, 2))
    sizes = (n_dp, n_group, n_tensor, heads_here, s_heads, images, tokens)
    dma = pltpu.SemaphoreType.DMA
    one = (heads_here, max(n_x - 1, 1))
    two = one + (max(n_group - 1, 1),)
    return pl.pallas_call(
        functools.partial(teacher_kernel, sizes),
        out_shape=jax.ShapeDtypeStruct((s_here, images, pad, QROWS), jnp.bfloat16),
        in_specs=[
            pl.BlockSpec(memory_space=pltpu.SMEM),
            pl.BlockSpec(memory_space=pltpu.VMEM),
            pl.BlockSpec(memory_space=pltpu.VMEM),
            pl.BlockSpec(memory_space=pl.ANY),
        ],
        out_specs=pl.BlockSpec(memory_space=pltpu.VMEM),
        scratch_shapes=[
            pltpu.VMEM((n_dp, 2, rows, width_here), jnp.bfloat16),
            pltpu.VMEM((images * pad, width), jnp.bfloat16),
            pltpu.VMEM((s_heads, images, pad, QROWS), jnp.float32),
            pltpu.VMEM((s_heads, images, pad, QROWS), jnp.bfloat16),
            pltpu.VMEM((max(n_tensor - 1, 1), s_here, images, pad, QROWS), jnp.bfloat16),
            dma,
            dma(one),
            dma(one),
            dma(two),
            dma(two),
            dma((heads_here,)),
            dma((heads_here,)),
            dma(one),
            dma(one),
            dma(two),
            dma(two),
            dma((max(n_tensor - 1, 1),)),
            dma((max(n_tensor - 1, 1),)),
        ],
        compiler_params=pltpu.CompilerParams(
            collective_id=0, has_side_effects=True, vmem_limit_bytes=67043328
        ),
    )(head_counts, teacher_input, teacher_gain.reshape(1, width), split)


def sum_over_dp(local, n_dp):
    half = local.shape[0] // CORES
    core = lax.rem(lax.axis_index("dp"), CORES)
    mates = [(d, d ^ 1) for d in range(n_dp)]
    rounded = local.astype(jnp.bfloat16)
    mine = lax.dynamic_slice_in_dim(local, core * half, half, 0)
    other = lax.dynamic_slice_in_dim(rounded, (1 - core) * half, half, 0)
    mine = mine + lax.ppermute(other, "dp", mates).astype(jnp.float32)
    sent = mine.astype(jnp.bfloat16)
    for s in range(1, n_dp // CORES):
        around = [(d, (d + CORES * s) % n_dp) for d in range(n_dp)]
        mine = mine + lax.ppermute(sent, "dp", around).astype(jnp.float32)
    done = mine.astype(jnp.bfloat16)
    theirs = lax.ppermute(done, "dp", mates)
    first = jnp.where(core == 0, done, theirs)
    second = jnp.where(core == 0, theirs, done)
    return jnp.concatenate([first, second], axis=0).astype(jnp.float32)


def on_device(
    mesh_sizes,
    teacher_input,
    teacher_gain,
    teacher_weight,
    head_counts,
    assignment,
    student_input,
    student_gain,
    student_bias,
    student_weight,
):
    images, tokens, width_s = student_input.shape
    student_heads = student_weight.shape[1] // (2 * HD_S)
    folded = teacher_folded(mesh_sizes, teacher_input, teacher_gain, teacher_weight, head_counts)
    piece = lax.all_gather(folded, "dp", axis=1, tiled=True)
    width_piece = piece.shape[1]
    positions = jnp.arange(width_piece, dtype=jnp.int32)
    picker = (assignment[:, None] == positions[None, :]).astype(jnp.bfloat16)
    target = jnp.einsum("ji,hikq->hjkq", picker, piece, preferred_element_type=jnp.float32)
    target_wide = target.astype(jnp.bfloat16).astype(jnp.float32)[:, :, :tokens]
    student_normed = layer_norm(student_input, student_gain, student_bias).astype(jnp.bfloat16)
    normed_front = student_normed[:, :QROWS]
    packed = student_weight.reshape(width_s, student_heads, 2, HD_S)
    weight_query = packed[:, :, 0, :].reshape(width_s, student_heads * HD_S)
    weight_key = packed[:, :, 1, :].reshape(width_s, student_heads * HD_S)
    student_query = (
        jnp.einsum("btd,dc->btc", normed_front, weight_query, preferred_element_type=jnp.float32)
        * HD_S ** (-0.5)
    ).astype(jnp.bfloat16)
    student_keys = jnp.einsum(
        "btd,dc->btc", student_normed, weight_key, preferred_element_type=jnp.float32
    ).astype(jnp.bfloat16)
    split_query = student_query.reshape(images, QROWS, student_heads, HD_S)
    split_keys = student_keys.reshape(images, tokens, student_heads, HD_S)
    probs = jax.nn.softmax(
        jnp.einsum("bqhd,bkhd->hbkq", split_query, split_keys, preferred_element_type=jnp.float32),
        axis=2,
    )
    score_grad = (probs * jnp.sum(target_wide, axis=2, keepdims=True) - target_wide).astype(
        jnp.bfloat16
    )
    query_grad = (
        jnp.einsum("hbkq,bkhd->bqhd", score_grad, split_keys, preferred_element_type=jnp.float32)
        * HD_S ** (-0.5)
    ).astype(jnp.bfloat16)
    key_grad = jnp.einsum(
        "hbkq,bqhd->bkhd", score_grad, split_query, preferred_element_type=jnp.float32
    ).astype(jnp.bfloat16)
    grad_query = jnp.einsum(
        "fkm,fkp->mp",
        normed_front,
        query_grad.reshape(images, QROWS, student_heads * HD_S),
        preferred_element_type=jnp.float32,
    )
    grad_key = jnp.einsum(
        "oip,ois->ps",
        student_normed,
        key_grad.reshape(images, tokens, student_heads * HD_S),
        preferred_element_type=jnp.float32,
    )
    local_grad = jnp.stack(
        [
            grad_query.reshape(width_s, student_heads, HD_S),
            grad_key.reshape(width_s, student_heads, HD_S),
        ],
        axis=2,
    )
    local_grad = local_grad.reshape(width_s, student_heads * 2 * HD_S)
    return sum_over_dp(local_grad, mesh_sizes[0])


def solution(mesh):
    placed = (
        P(("group", "dp"), None, None),
        P(),
        P("dp", None, "tensor"),
        P(),
        P(("group", "dp")),
        P(("group", "dp"), None, None),
        P(),
        P(),
        P(None, "tensor"),
    )
    mesh_sizes = (mesh.shape["dp"], mesh.shape["group"], mesh.shape["tensor"])
    return jax.shard_map(
        functools.partial(on_device, mesh_sizes),
        mesh=mesh,
        in_specs=placed,
        out_specs=P("group", "tensor"),
        check_vma=False,
    )
```

time: 449 us -> 264 us (0.59)
  waiting for transfers between devices: 341 us -> 35.6 us
  Pallas kernels: 0 us -> 178 us
  matrix products: 36.8 us -> 11 us
  local copies, waits for them, and re-layouts: 40.2 us -> 22.1 us
  other arithmetic: 17.1 us -> 3.23 us
    all_gather x1 -> x0, waiting for transfers between devices: 202 us -> none  [on_device(): piece = lax.all_gather(teacher_weight, 'dp', axis=0, tiled=True)]
    pallas_call x0 -> x1, Pallas kernels: none -> 178 us  [teacher_folded(): pl.pallas_call(functools.partial(teacher_kernel, sizes), out_shape=jax.Sh...]
    unnamed x5 -> x1, waiting for transfers between devices: 85.8 us -> 0.02 us
    psum x1 -> x0, waiting for transfers between devices: 36.5 us -> none  [on_device(): return lax.psum(local_grad.astype(jnp.bfloat16), 'dp').astype(jnp.float32)]
    dot_general x5 -> x1, matrix products: 29.9 us -> 2.42 us  [on_device(): jnp.einsum('ji,hikq->hjkq', picker, piece, preferred_element_type=jnp.flo...]
    ppermute x0 -> x3, waiting for transfers between devices: none -> 17.3 us  [the longest x1 13.7 us: sum_over_dp(): mine = mine + lax.ppermute(sent, 'dp', around).astype(jnp.float32)]
    reshape x3 -> x0, local copies, waits for them, and re-layouts: 14.6 us -> none  [the longest x1 9.77 us: on_device(): normed_keys = teacher_normed.reshape(images * tokens, width_t)]
    reduce_sum x2 -> x1, other arithmetic: 6.6 us -> 0.3 us  [layer_norm(): center = wide - jnp.mean(wide, axis=-1, keepdims=True)]
  transfers between devices with their start and end apart: 4 -> 4, of which waited for: 4 -> 4; matrix products, arithmetic and copies ran while one was open for 6% -> 2% of each run, Pallas kernels for 0% -> 0%
where the time goes in v1:
time: 264 us
  Pallas kernels  178 us (67%)
  waiting for transfers between devices  35.6 us (13%)
  local copies, waits for them, and re-layouts  22.1 us (8%)
  between operations  13.6 us (5%)
  matrix products  11 us (4%)
  other arithmetic  3.23 us (1%)
    pallas_call x1, Pallas kernels, teacher_folded(): pl.pallas_call(functools.partial(teacher_kernel, sizes), out_shape=jax.Sh...  178 us
    unnamed x16, local copies, waits for them, and re-layouts  19.4 us
    all_gather x1, waiting for transfers between devices, on_device(): piece = lax.all_gather(folded, 'dp', axis=1, tiled=True)  18.3 us
    ppermute x1, waiting for transfers between devices, sum_over_dp(): mine = mine + lax.ppermute(sent, 'dp', around).astype(jnp.float32)  13.7 us
  transfers between devices with their start and end apart: 4, of which 4 were waited for; matrix products, arithmetic and copies ran while one was open for 2% of the time, Pallas kernels for 0%

profile of v1, /device:TPU:0, one launch (start us, length us, event | category | flops | bytes accessed | tf_op | source)
XLA Modules:
  0.0 263.8 jit_solution(7698314906714365036)
XLA Ops:
  6.5 8.8 %copy.81 = bf16[1536,2,1536]{2,0,1:T(8,128)(2,1)} copy(bf16[1536,2,1536]{2,1,0:T(2,128)(2,1)} %param.11) | data formatting | bytes 18874368 | tf_op args[2]
  15.3 8.2 %copy.34.x_ref = bf16[2,257,6144]{2,1,0:T(8,128)(2,1)} copy(bf16[2,257,6144]{2,0,1:T(2,128)(2,1)} %param.9) | data formatting | bytes 12632064 | tf_op args[0]
  23.5 0.7 copy.33.counts_ref
  24.2 177.6 %shard_map.91 = bf16[4,2,272,128]{3,2,1,0:T(8,128)(2,1)} custom-call(s32[48,16]{1,0:T(8,128)} %copy.33.counts_ref, bf16[2,257,6144]{2,1,0:T(8,128)(2,1)} %copy.34.x_ref, f32[1,6144]{1,0:T(1,128)} %bitcast.83, bf16[2,1536,1536]{2,1,0:T(8,128)(2,1)} %bitcast.70), custom_call_target="tpu_custom_call" | custom-call | tf_op jit(solution)/shard_map/pallas_call | solution.py:288
  201.8 1.7 copy.25
  203.6 0.3 convert_reduce_fusion
  203.9 0.5 fusion.7
  204.5 0.5 fusion.10
  205.0 0.3 fusion.19
  205.3 0.1 copy.29
  205.5 0.8 convolution_convert_fusion.1
  206.3 0.2 copy.27
  206.5 18.3 %all-gather.2.cloned.1.call-done = bf16[4,8,272,128]{3,2,1,0:T(8,128)(2,1)} async-done(((bf16[4,2,272,128]{3,2,1,0:T(8,128)(2,1)}), bf16[4,8,272,128]{3,2,1,0:T(8,128)(2,1)}) %all-gather.2.cloned.1.call-update) | async-done | bytes 2228240 | tf_op jit(solution)/shard_map/all_gather | solution.py:358
  224.8 2.4 fusion.5
  227.2 0.1 copy.82
  227.3 1.1 fusion
  228.4 2.8 %fusion.17 = bf16[4,2,257,128]{3,2,1,0:T(8,128)(2,1)} fusion(f32[4,2,257,128]{3,2,1,0:T(8,128)} %fusion, bf16[4,2,272,128]{3,2,1,0:T(8,128)(2,1)S(1)} %bitcast.76, bf16[2,257,4,64]{1,3,2,0:T(8,128)(2,1)S(1)} %bitcast.79, bf16[2,128,4,64]{1,3,2,0:T(8,128)(2,1)S(1)} %bitcast.81), kind=kOutput, calls=%fused_computation.24 | convolution fusion | flops 35267072 | bytes 2499584 | tf_op jit(solution)/shard_map/div | solution.py:378
  231.2 2.5 convolution_bitcast_fusion
  233.7 2.1 convolution_bitcast_fusion.1
  235.9 0.1 pad_maximum_fusion
  236.0 0.2 copy.41
  236.3 0.1 dynamic-slice_convert_fusion
  236.4 0.3 collective-permute-start
  236.7 1.7 collective-permute-done
  238.3 0.2 fusion.23
  238.5 0.4 collective-permute-start.1
  238.9 13.7 %collective-permute-done.1 = bf16[512,512]{0,1:T(8,128)(2,1)S(1)} collective-permute-done((bf16[512,512]{0,1:T(8,128)(2,1)S(1)}, bf16[512,512]{0,1:T(8,128)(2,1)S(1)}, u32[]{:S(2)}, u32[]{:S(2)}) %collective-permute-start.1) | collective-permute-done | bytes 524320 | tf_op jit(solution)/shard_map/ppermute | solution.py:335
  252.6 0.2 add_convert_fusion
  252.9 1.9 collective-permute-done.2
  254.8 0.1 broadcast_select_fusion.1
  254.9 0.3 maximum_convert_fusion
  255.2 1.8 copy.42
  (18 shorter events, 0.2 us)
Async XLA Ops:
  6.5 218.3 %all-gather.2.cloned.1.call-start = ((), (), s32[]{:S(2)}) async-start(), calls=%async_computation | async-start | bytes 2785280 | tf_op jit(solution)/shard_map/all_gather | solution.py:358
  15.3 8.2 %copy-start.2 = (s32[48,16]{0,1:T(8,128)S(1)}, s32[48,16]{0,1:T(8,128)}, u32[]{:S(2)}) copy-start(s32[48,16]{0,1:T(8,128)} %param.12) | copy-start | bytes 9220
  201.8 1.8 copy-start
  203.6 0.9 copy-start.3
  203.6 0.9 copy-start.4
  205.5 19.3 %copy-start.5 = (s32[2]{0:T(128)S(1)}, s32[2]{0:T(128)}, u32[]{:S(2)}) copy-start(s32[2]{0:T(128)} %param.13) | copy-start | bytes 28
  233.7 2.1 copy-start.1
  236.4 2.0 collective-permute-start
  238.5 14.1 %collective-permute-start.1 = (bf16[512,512]{0,1:T(8,128)(2,1)S(1)}, bf16[512,512]{0,1:T(8,128)(2,1)S(1)}, u32[]{:S(2)}, u32[]{:S(2)}) collective-permute-start(bf16[512,512]{0,1:T(8,128)(2,1)S(1)} %fusion.23), channel_id=1, source_target_pairs={{0,2},{1,3},{2,0},{3,1},{4,6},{5,7},{6,4},{7,5},{8,10},{9,11},{10,... | collective-permute-start | bytes 1572872 | tf_op jit(solution)/shard_map/ppermute | solution.py:335
  252.9 2.0 collective-permute-start.2
Sparse Core Ops, SparseCore 0:
  201.9 22.8 all-gather.1

commit v2 on v1

--- a/solution.py
+++ b/solution.py
@@ -29,6 +29,7 @@
 def teacher_kernel(
     sizes,
     counts_ref,
+    slots_ref,
     x_ref,
     gain_ref,
     w_ref,
@@ -38,6 +39,7 @@
     acc,
     part,
     landed,
+    gathered,
     own_sem,
     sx,
     rx,
@@ -51,6 +53,8 @@
     rpy,
     sz,
     rz,
+    sg,
+    rg,
 ):
     n_dp, n_group, n_tensor, heads_here, s_heads, images, tokens = sizes
     n_x = n_dp // CORES
@@ -74,11 +78,11 @@
 
     barrier = pltpu.get_barrier_semaphore()
     waits = 0
-    for s in range(1, n_x):
-        pl.semaphore_signal(barrier, inc=1, device_id={"dp": x_peer(s)}, device_id_type=MESH)
+    for s in range(1, n_dp):
+        pl.semaphore_signal(
+            barrier, inc=1, device_id={"dp": lax.rem(dp + s, n_dp)}, device_id_type=MESH
+        )
         waits += 1
-    pl.semaphore_signal(barrier, inc=1, device_id={"dp": mate}, device_id_type=MESH)
-    waits += 1
     for s in range(1, n_group):
         pl.semaphore_signal(
             barrier, inc=1, device_id={"group": lax.rem(y + s, n_group)}, device_id_type=MESH
@@ -160,8 +164,11 @@
     own_copy = pltpu.make_async_copy(w_ref, wbuf.at[dp], own_sem)
     own_copy.start()
 
-    gain = gain_ref[...]
-    for i in range(images):
+    acc[...] = jnp.zeros_like(acc)
+    own_copy.wait()
+
+    def norm_image(i):
+        gain = gain_ref[...]
 
         def norm_rows(r, carry):
             block = layer_norm(x_ref[i, pl.ds(pl.multiple_of(r * 16, 16), 16), :], gain, 0.0)
@@ -173,11 +180,9 @@
         rest = tokens - whole * 16
         if rest:
             last = layer_norm(x_ref[i, whole * 16 : tokens, :], gain, 0.0)
-            normed[i * pad + whole * 16 : (i + 1) * pad, :] = jnp.concatenate(
+            normed[pl.ds(pl.multiple_of(i * pad + whole * 16, 16), 16), :] = jnp.concatenate(
                 [last, jnp.zeros((16 - rest, last.shape[1]), jnp.float32)], axis=0
             ).astype(jnp.bfloat16)
-    acc[...] = jnp.zeros_like(acc)
-    own_copy.wait()
 
     def attend(k):
         keys = jnp.zeros((images * pad, HD_T), jnp.float32)
@@ -225,31 +230,62 @@
                 for g in range(1, n_group):
                     copy_y(j, s, g).wait_recv()
                     copy_mate_y(j, s, g).start()
+
+        @pl.when(k < images)
+        def _():
+            norm_image(k)
+
+        def ready(j, inner):
             copy_own(j).wait_recv()
             for s in range(1, n_x):
                 copy_mate_x(j, s).wait_recv()
                 for g in range(1, n_group):
                     copy_mate_y(j, s, g).wait_recv()
             attend(j)
-
+            return inner
+
+        lax.fori_loop(
+            jnp.where(k <= images, 0, k - 1), jnp.where(k < images, 0, k), ready, 0
+        )
         return carry
 
     lax.fori_loop(0, heads_here + 1, step, 0)
 
-    def copy_z(s):
+    def copy_z(s, h):
         to = lax.rem(t + s, n_tensor)
         return pltpu.make_async_remote_copy(
-            src_ref=part.at[pl.ds(to * s_here, s_here)],
-            dst_ref=landed.at[s - 1],
-            send_sem=sz.at[s - 1],
-            recv_sem=rz.at[s - 1],
+            src_ref=part.at[to * s_here + h],
+            dst_ref=landed.at[s - 1, h],
+            send_sem=sz.at[s - 1, h],
+            recv_sem=rz.at[s - 1, h],
             device_id={"tensor": to},
             device_id_type=MESH,
         )
 
-    part[...] = (acc[...] / DIVISOR).astype(jnp.bfloat16)
-    for s in range(n_tensor - 1, 0, -1):
-        copy_z(s).start()
+    def copy_dp(s, h):
+        own = gathered.at[h, pl.ds(dp * images, images)]
+        return pltpu.make_async_remote_copy(
+            src_ref=own,
+            dst_ref=own,
+            send_sem=sg.at[s - 1, h],
+            recv_sem=rg.at[s - 1, h],
+            device_id={"dp": lax.rem(dp + s, n_dp)},
+            device_id_type=MESH,
+        )
+
+    for h in range(s_here):
+        for s in range(1, n_tensor):
+            spot = lax.rem(t + s, n_tensor) * s_here + h
+            part[spot] = (acc[spot] / DIVISOR).astype(jnp.bfloat16)
+            copy_z(s, h).start()
+    for h in range(s_here):
+        total = (acc[t * s_here + h] / DIVISOR).astype(jnp.bfloat16).astype(jnp.float32)
+        for s in range(1, n_tensor):
+            copy_z(s, h).wait_recv()
+            total += landed[s - 1, h].astype(jnp.float32)
+        gathered[h, pl.ds(dp * images, images)] = total.astype(jnp.bfloat16)
+        for s in range(1, n_dp):
+            copy_dp(s, h).start()
 
     def drain(k, carry):
         for s in range(1, n_x):
@@ -262,16 +298,17 @@
         return carry
 
     lax.fori_loop(0, heads_here, drain, 0)
-    for s in range(1, n_tensor):
-        copy_z(s).wait()
     for h in range(s_here):
-        total = part[t * s_here + h].astype(jnp.float32)
         for s in range(1, n_tensor):
-            total += landed[s - 1, h].astype(jnp.float32)
-        out_ref[h] = total.astype(jnp.bfloat16)
-
-
-def teacher_folded(mesh_sizes, teacher_input, teacher_gain, teacher_weight, head_counts):
+            copy_z(s, h).wait_send()
+        for s in range(1, n_dp):
+            copy_dp(s, h).wait()
+    for h in range(s_here):
+        for j in range(images):
+            out_ref[h, j] = gathered[h, slots_ref[j]]
+
+
+def teacher_folded(mesh_sizes, teacher_input, teacher_gain, teacher_weight, head_counts, assignment):
     n_dp, n_group, n_tensor = mesh_sizes
     images, tokens, width = teacher_input.shape
     rows, _, width_here = teacher_weight.shape
@@ -290,6 +327,7 @@
         out_shape=jax.ShapeDtypeStruct((s_here, images, pad, QROWS), jnp.bfloat16),
         in_specs=[
             pl.BlockSpec(memory_space=pltpu.SMEM),
+            pl.BlockSpec(memory_space=pltpu.SMEM),
             pl.BlockSpec(memory_space=pltpu.VMEM),
             pl.BlockSpec(memory_space=pltpu.VMEM),
             pl.BlockSpec(memory_space=pl.ANY),
@@ -301,6 +339,7 @@
             pltpu.VMEM((s_heads, images, pad, QROWS), jnp.float32),
             pltpu.VMEM((s_heads, images, pad, QROWS), jnp.bfloat16),
             pltpu.VMEM((max(n_tensor - 1, 1), s_here, images, pad, QROWS), jnp.bfloat16),
+            pltpu.VMEM((s_here, n_dp * images, pad, QROWS), jnp.bfloat16),
             dma,
             dma(one),
             dma(one),
@@ -312,13 +351,15 @@
             dma(one),
             dma(two),
             dma(two),
-            dma((max(n_tensor - 1, 1),)),
-            dma((max(n_tensor - 1, 1),)),
+            dma((max(n_tensor - 1, 1), s_here)),
+            dma((max(n_tensor - 1, 1), s_here)),
+            dma((n_dp - 1, s_here)),
+            dma((n_dp - 1, s_here)),
         ],
         compiler_params=pltpu.CompilerParams(
             collective_id=0, has_side_effects=True, vmem_limit_bytes=67043328
         ),
-    )(head_counts, teacher_input, teacher_gain.reshape(1, width), split)
+    )(head_counts, assignment, teacher_input, teacher_gain.reshape(1, width), split)
 
 
 def sum_over_dp(local, n_dp):
@@ -354,13 +395,10 @@
 ):
     images, tokens, width_s = student_input.shape
     student_heads = student_weight.shape[1] // (2 * HD_S)
-    folded = teacher_folded(mesh_sizes, teacher_input, teacher_gain, teacher_weight, head_counts)
-    piece = lax.all_gather(folded, "dp", axis=1, tiled=True)
-    width_piece = piece.shape[1]
-    positions = jnp.arange(width_piece, dtype=jnp.int32)
-    picker = (assignment[:, None] == positions[None, :]).astype(jnp.bfloat16)
-    target = jnp.einsum("ji,hikq->hjkq", picker, piece, preferred_element_type=jnp.float32)
-    target_wide = target.astype(jnp.bfloat16).astype(jnp.float32)[:, :, :tokens]
+    target = teacher_folded(
+        mesh_sizes, teacher_input, teacher_gain, teacher_weight, head_counts, assignment
+    )
+    target_wide = target.astype(jnp.float32)[:, :, :tokens]
     student_normed = layer_norm(student_input, student_gain, student_bias).astype(jnp.bfloat16)
     normed_front = student_normed[:, :QROWS]
     packed = student_weight.reshape(width_s, student_heads, 2, HD_S)

time: 264 us -> 239 us (0.905)
  waiting for transfers between devices: 35.6 us -> 17.1 us
  between operations: 13.6 us -> 0.29 us
  matrix products: 11 us -> 6.89 us
  other arithmetic: 3.23 us -> 5.92 us
    all_gather x1 -> x0, waiting for transfers between devices: 18.3 us -> none  [on_device(): piece = lax.all_gather(folded, 'dp', axis=1, tiled=True)]
    pallas_call x1, Pallas kernels: 178 us -> 180 us  [teacher_folded(): pl.pallas_call(functools.partial(teacher_kernel, sizes), out_shape=jax.Sh...]
    unnamed x16 -> x36, local copies, waits for them, and re-layouts: 19.4 us -> 20.6 us
  transfers between devices with their start and end apart: 4 -> 3, of which waited for: 4 -> 3; matrix products, arithmetic and copies ran while one was open for 2% -> 0% of each run, Pallas kernels for 0% -> 0%
where the time goes in v2:
time: 239 us; the launch traced here: 237 us
  Pallas kernels  180 us (75%)
  local copies, waits for them, and re-layouts  24.5 us (10%)
  waiting for transfers between devices  17.1 us (7%)
  matrix products  6.89 us (3%)
  other arithmetic  5.92 us (2%)
  starting transfers between devices  2.48 us (1%)
    pallas_call x1, Pallas kernels, teacher_folded(): pl.pallas_call(functools.partial(teacher_kernel, sizes), out_shape=jax.Sh...  180 us
    unnamed x36, local copies, waits for them, and re-layouts  20.6 us
    ppermute x1, waiting for transfers between devices, sum_over_dp(): mine = mine + lax.ppermute(sent, 'dp', around).astype(jnp.float32)  13.7 us
  transfers between devices with their start and end apart: 3, of which 3 were waited for; matrix products, arithmetic and copies ran while one was open for 0% of the time, Pallas kernels for 0%

profile of v2, /device:TPU:0, one launch (start us, length us, event | category | flops | bytes accessed | tf_op | source)
XLA Modules:
  0.0 237.4 jit_solution(10770834443855042107)
XLA Ops:
  0.0 1.6 convert_reduce_fusion
  1.6 1.7 fusion.5
  3.4 0.5 copy.23
  3.9 0.1 fusion.41
  4.0 0.6 copy-done
  4.6 0.5 fusion.8
  5.1 1.0 copy-done.2
  6.1 0.3 fusion.17
  6.4 0.8 copy.27
  7.2 0.8 convolution_convert_fusion.1
  8.0 0.9 copy.25
  9.0 8.8 %copy.71 = bf16[1536,2,1536]{2,0,1:T(8,128)(2,1)} copy(bf16[1536,2,1536]{2,1,0:T(2,128)(2,1)} %param.11) | data formatting | bytes 18874368 | tf_op args[2]
  17.7 8.2 %copy.32.x_ref = bf16[2,257,6144]{2,1,0:T(8,128)(2,1)} copy(bf16[2,257,6144]{2,0,1:T(2,128)(2,1)} %param.9) | data formatting | bytes 12632064 | tf_op args[0]
  25.9 0.7 copy.31.counts_ref
  26.6 180.2 %shard_map.91 = bf16[4,2,272,128]{3,2,1,0:T(8,128)(2,1)} custom-call(s32[48,16]{1,0:T(8,128)} %copy.31.counts_ref, s32[2]{0:T(128)} %slots_ref.1, bf16[2,257,6144]{2,1,0:T(8,128)(2,1)} %copy.32.x_ref, f32[1,6144]{1,0:T(1,128)} %bitcast.73, bf16[2,1536,1536]{2,1,0:T(8,128)(2,1)} %bitcast.62), custom_call_target="tpu_custom_call" | custom-call | tf_op jit(solution)/shard_map/pallas_call | solution.py:325
  206.8 1.2 fusion
  208.0 2.1 fusion.15
  210.1 0.8 copy-done.15
  211.0 1.6 convolution_bitcast_fusion
  212.6 2.0 convolution_bitcast_fusion.1
  214.7 0.2 pad_maximum_fusion
  214.9 0.2 copy.37
  215.2 0.1 dynamic-slice_convert_fusion
  215.3 1.8 collective-permute-start
  217.1 1.5 collective-permute-done
  218.6 0.2 fusion.21
  218.8 0.6 collective-permute-start.1
  219.4 13.7 %collective-permute-done.1 = bf16[512,512]{0,1:T(8,128)(2,1)S(1)} collective-permute-done((bf16[512,512]{0,1:T(8,128)(2,1)S(1)}, bf16[512,512]{0,1:T(8,128)(2,1)S(1)}, u32[]{:S(2)}, u32[]{:S(2)}) %collective-permute-start.1) | collective-permute-done | bytes 524320 | tf_op jit(solution)/shard_map/ppermute | solution.py:376
  233.1 0.2 add_convert_fusion
  233.4 1.9 collective-permute-done.2
  235.4 0.3 maximum_convert_fusion
  235.6 1.8 copy.38
  (33 shorter events, 0.2 us)
Async XLA Ops:
  0.0 3.3 %copy-start.3 = (bf16[1024,512]{1,0:T(8,128)(2,1)S(1)}, bf16[1024,512]{1,0:T(8,128)(2,1)}, u32[]{:S(2)}) copy-start(bf16[1024,512]{1,0:T(8,128)(2,1)} %param.17) | copy-start | bytes 3145732
  1.6 5.6 %copy-start.6 = (f32[2,257]{1,0:T(2,128)}, f32[2,257]{1,0:T(2,128)S(1)}, u32[]{:S(2)}) copy-start(f32[2,257]{1,0:T(2,128)S(1)} %broadcast_multiply_fusion) | copy-start | bytes 6172
  3.4 3.8 %copy-start.8 = (f32[2,257]{1,0:T(2,128)}, f32[2,257]{1,0:T(2,128)S(1)}, u32[]{:S(2)}) copy-start(f32[2,257]{1,0:T(2,128)S(1)} %add_rsqrt_fusion) | copy-start | bytes 6172
  3.4 1.2 copy-start
  3.4 1.2 copy-start.11
  3.4 1.2 copy-start.13
  5.1 1.0 copy-start.2
  17.7 8.2 %copy-start.10 = (s32[48,16]{0,1:T(8,128)S(1)}, s32[48,16]{0,1:T(8,128)}, u32[]{:S(2)}) copy-start(s32[48,16]{0,1:T(8,128)} %param.12) | copy-start | bytes 9220
  208.0 2.9 %copy-start.4 = (bf16[2,257,256]{1,2,0:T(8,128)(2,1)S(1)}, bf16[2,257,256]{1,2,0:T(8,128)(2,1)}, u32[]{:S(2)}) copy-start(bf16[2,257,256]{1,2,0:T(8,128)(2,1)} %copy.25) | copy-start | bytes 789508
  210.1 0.8 copy-start.15
  210.9 1.7 copy-start.1
  210.9 1.7 copy-start.5
  210.9 1.7 copy-start.7
  210.9 1.7 copy-start.9
  210.9 1.7 copy-start.12
  211.0 1.7 copy-start.14
  215.3 3.4 %collective-permute-start = (bf16[512,512]{0,1:T(8,128)(2,1)S(1)}, bf16[512,512]{0,1:T(8,128)(2,1)S(1)}, u32[]{:S(2)}, u32[]{:S(2)}) collective-permute-start(bf16[512,512]{0,1:T(8,128)(2,1)S(1)} %dynamic-slice_convert_fusion), channel_id=1, source_target_pairs={{0,1},{1,0},{2,3},{3,2},{4,5},{5,4},{6,7},{7,6},{8,9},{9,8},{10,11... | collective-permute-start | bytes 1572872 | tf_op jit(solution)/shard_map/ppermute | solution.py:372
  218.8 14.3 %collective-permute-start.1 = (bf16[512,512]{0,1:T(8,128)(2,1)S(1)}, bf16[512,512]{0,1:T(8,128)(2,1)S(1)}, u32[]{:S(2)}, u32[]{:S(2)}) collective-permute-start(bf16[512,512]{0,1:T(8,128)(2,1)S(1)} %fusion.21), channel_id=1, source_target_pairs={{0,2},{1,3},{2,0},{3,1},{4,6},{5,7},{6,4},{7,5},{8,10},{9,11},{10,... | collective-permute-start | bytes 1572872 | tf_op jit(solution)/shard_map/ppermute | solution.py:376
  233.3 2.0 collective-permute-start.2

commit v3 on v2

--- a/solution.py
+++ b/solution.py
@@ -36,10 +36,13 @@
     out_ref,
     wbuf,
     normed,
+    stage,
     acc,
-    part,
+    made,
     landed,
+    fold,
     gathered,
+    stage_sem,
     own_sem,
     sx,
     rx,
@@ -53,8 +56,12 @@
     rpy,
     sz,
     rz,
+    sf,
+    rf,
     sg,
     rg,
+    sm,
+    rm,
 ):
     n_dp, n_group, n_tensor, heads_here, s_heads, images, tokens = sizes
     n_x = n_dp // CORES
@@ -62,6 +69,8 @@
     rows_part = rows // n_group
     pad = normed.shape[0] // images
     s_here = s_heads // n_tensor
+    per_image = n_tensor // images
+    s_part = s_heads // per_image
 
     dp = lax.axis_index("dp")
     y = lax.axis_index("group")
@@ -69,6 +78,8 @@
     x = dp // CORES
     core = lax.rem(dp, CORES)
     mate = x * CORES + (1 - core)
+    my_image = t // per_image
+    my_part = lax.rem(t, per_image)
 
     def x_peer(s):
         return lax.rem(x + s, n_x) * CORES + core
@@ -169,9 +180,12 @@
 
     def norm_image(i):
         gain = gain_ref[...]
+        fetch = pltpu.make_async_copy(x_ref.at[i], stage, stage_sem)
+        fetch.start()
+        fetch.wait()
 
         def norm_rows(r, carry):
-            block = layer_norm(x_ref[i, pl.ds(pl.multiple_of(r * 16, 16), 16), :], gain, 0.0)
+            block = layer_norm(stage[pl.ds(pl.multiple_of(r * 16, 16), 16), :], gain, 0.0)
             normed[pl.ds(pl.multiple_of(i * pad + r * 16, 16), 16), :] = block.astype(jnp.bfloat16)
             return carry
 
@@ -179,12 +193,23 @@
         lax.fori_loop(0, whole, norm_rows, 0)
         rest = tokens - whole * 16
         if rest:
-            last = layer_norm(x_ref[i, whole * 16 : tokens, :], gain, 0.0)
+            last = layer_norm(stage[whole * 16 : tokens, :], gain, 0.0)
             normed[pl.ds(pl.multiple_of(i * pad + whole * 16, 16), 16), :] = jnp.concatenate(
                 [last, jnp.zeros((16 - rest, last.shape[1]), jnp.float32)], axis=0
             ).astype(jnp.bfloat16)
 
-    def attend(k):
+    def copy_z(k, s):
+        to = lax.rem(t + s, n_tensor)
+        return pltpu.make_async_remote_copy(
+            src_ref=made.at[k, to // per_image],
+            dst_ref=landed.at[s - 1, k],
+            send_sem=sz.at[k, s - 1],
+            recv_sem=rz.at[k, s - 1],
+            device_id={"tensor": to},
+            device_id_type=MESH,
+        )
+
+    def project(k):
         keys = jnp.zeros((images * pad, HD_T), jnp.float32)
         query = jnp.zeros((images * QROWS, HD_T), jnp.float32)
         for d in range(n_dp):
@@ -199,20 +224,30 @@
         query = (query * HD_T ** (-0.5)).astype(jnp.bfloat16)
         keys = keys.astype(jnp.bfloat16)
         for i in range(images):
+            made[k, i, :pad] = keys[i * pad : (i + 1) * pad]
+            made[k, i, pad:] = query[i * QROWS : (i + 1) * QROWS]
+        for s in range(1, n_tensor):
+            copy_z(k, s).start()
+
+    def attend(k):
+        for s in range(n_tensor):
+            if s:
+                copy_z(k, s).wait_recv()
+                keys, query = landed[s - 1, k, :pad], landed[s - 1, k, pad:]
+            else:
+                keys, query = made[k, my_image, :pad], made[k, my_image, pad:]
             scores = lax.dot_general(
-                keys[i * pad : (i + 1) * pad],
-                query[i * QROWS : (i + 1) * QROWS],
-                (((1,), (1,)), ((), ())),
-                preferred_element_type=jnp.float32,
+                keys, query, (((1,), (1,)), ((), ())), preferred_element_type=jnp.float32
             )
             spot = lax.broadcasted_iota(jnp.int32, scores.shape, 0)
             scores = jnp.where(spot < tokens, scores, -jnp.inf)
             power = jnp.exp(scores - jnp.max(scores, axis=0, keepdims=True))
             maps = power / jnp.sum(power, axis=0, keepdims=True)
             maps = maps.astype(jnp.bfloat16).astype(jnp.float32)
-            for s in range(s_heads):
-                count = counts_ref[t * heads_here + k, s].astype(jnp.float32)
-                acc[s, i] += count * maps
+            head = lax.rem(t + n_tensor - s, n_tensor) * heads_here + k
+            for h in range(s_part):
+                count = counts_ref[head, my_part * s_part + h].astype(jnp.float32)
+                acc[s, h] += count * maps
 
     def step(k, carry):
         @pl.when(k < heads_here)
@@ -241,7 +276,12 @@
                 copy_mate_x(j, s).wait_recv()
                 for g in range(1, n_group):
                     copy_mate_y(j, s, g).wait_recv()
-            attend(j)
+            project(j)
+
+            @pl.when(j > 0)
+            def _():
+                attend(j - 1)
+
             return inner
 
         lax.fori_loop(
@@ -251,14 +291,25 @@
 
     lax.fori_loop(0, heads_here + 1, step, 0)
 
-    def copy_z(s, h):
-        to = lax.rem(t + s, n_tensor)
-        return pltpu.make_async_remote_copy(
-            src_ref=part.at[to * s_here + h],
-            dst_ref=landed.at[s - 1, h],
-            send_sem=sz.at[s - 1, h],
-            recv_sem=rz.at[s - 1, h],
-            device_id={"tensor": to},
+    attend(heads_here - 1)
+
+    def copy_fold(w, h):
+        return pltpu.make_async_remote_copy(
+            src_ref=fold.at[w * s_here + h],
+            dst_ref=gathered.at[h, dp * images + my_image],
+            send_sem=sf.at[w, h],
+            recv_sem=rf.at[my_image, h],
+            device_id={"tensor": my_part * images + w},
+            device_id_type=MESH,
+        )
+
+    def arrived_fold(i, h):
+        return pltpu.make_async_remote_copy(
+            src_ref=fold.at[h],
+            dst_ref=gathered.at[h, dp * images + i],
+            send_sem=sf.at[0, h],
+            recv_sem=rf.at[i, h],
+            device_id={"tensor": i * per_image + t // images},
             device_id_type=MESH,
         )
 
@@ -269,23 +320,52 @@
             dst_ref=own,
             send_sem=sg.at[s - 1, h],
             recv_sem=rg.at[s - 1, h],
-            device_id={"dp": lax.rem(dp + s, n_dp)},
+            device_id={"dp": x_peer(s)},
+            device_id_type=MESH,
+        )
+
+    def copy_mate(s, h):
+        block = gathered.at[h, pl.ds(x_source(s) * images, images)]
+        return pltpu.make_async_remote_copy(
+            src_ref=block,
+            dst_ref=block,
+            send_sem=sm.at[s, h],
+            recv_sem=rm.at[s, h],
+            device_id={"dp": mate},
             device_id_type=MESH,
         )
 
     for h in range(s_here):
-        for s in range(1, n_tensor):
-            spot = lax.rem(t + s, n_tensor) * s_here + h
-            part[spot] = (acc[spot] / DIVISOR).astype(jnp.bfloat16)
-            copy_z(s, h).start()
+        for w in range(images):
+            spot = w * s_here + h
+            total = jnp.zeros((pad, QROWS), jnp.float32)
+            for s in range(n_tensor):
+                total += (acc[s, spot] / DIVISOR).astype(jnp.bfloat16).astype(jnp.float32)
+            total = total.astype(jnp.bfloat16)
+            fold[spot] = total
+
+            @pl.when(my_part * images + w != t)
+            def _():
+                copy_fold(w, h).start()
+
+            @pl.when(my_part * images + w == t)
+            def _():
+                gathered[h, dp * images + my_image] = total
+
     for h in range(s_here):
-        total = (acc[t * s_here + h] / DIVISOR).astype(jnp.bfloat16).astype(jnp.float32)
-        for s in range(1, n_tensor):
-            copy_z(s, h).wait_recv()
-            total += landed[s - 1, h].astype(jnp.float32)
-        gathered[h, pl.ds(dp * images, images)] = total.astype(jnp.bfloat16)
-        for s in range(1, n_dp):
+        for i in range(images):
+
+            @pl.when(i * per_image + t // images != t)
+            def _():
+                arrived_fold(i, h).wait_recv()
+
+        for s in range(1, n_x):
             copy_dp(s, h).start()
+        copy_mate(0, h).start()
+    for h in range(s_here):
+        for s in range(1, n_x):
+            copy_dp(s, h).wait_recv()
+            copy_mate(s, h).start()
 
     def drain(k, carry):
         for s in range(1, n_x):
@@ -295,14 +375,22 @@
                 copy_y(k, s, g).wait_send()
                 copy_mate_y(k, s, g).wait_send()
         copy_own(k).wait_send()
+        for s in range(1, n_tensor):
+            copy_z(k, s).wait_send()
         return carry
 
     lax.fori_loop(0, heads_here, drain, 0)
     for h in range(s_here):
-        for s in range(1, n_tensor):
-            copy_z(s, h).wait_send()
-        for s in range(1, n_dp):
-            copy_dp(s, h).wait()
+        for w in range(images):
+
+            @pl.when(my_part * images + w != t)
+            def _():
+                copy_fold(w, h).wait_send()
+
+        for s in range(1, n_x):
+            copy_dp(s, h).wait_send()
+        for s in range(n_x):
+            copy_mate(s, h).wait()
     for h in range(s_here):
         for j in range(images):
             out_ref[h, j] = gathered[h, slots_ref[j]]
@@ -317,6 +405,7 @@
     s_here = s_heads // n_tensor
     pad = rounded_up(tokens, 16)
     n_x = n_dp // CORES
+    s_part = s_heads * images // n_tensor
     split = jnp.transpose(teacher_weight, (1, 0, 2))
     sizes = (n_dp, n_group, n_tensor, heads_here, s_heads, images, tokens)
     dma = pltpu.SemaphoreType.DMA
@@ -328,7 +417,7 @@
         in_specs=[
             pl.BlockSpec(memory_space=pltpu.SMEM),
             pl.BlockSpec(memory_space=pltpu.SMEM),
-            pl.BlockSpec(memory_space=pltpu.VMEM),
+            pl.BlockSpec(memory_space=pl.ANY),
             pl.BlockSpec(memory_space=pltpu.VMEM),
             pl.BlockSpec(memory_space=pl.ANY),
         ],
@@ -336,10 +425,13 @@
         scratch_shapes=[
             pltpu.VMEM((n_dp, 2, rows, width_here), jnp.bfloat16),
             pltpu.VMEM((images * pad, width), jnp.bfloat16),
-            pltpu.VMEM((s_heads, images, pad, QROWS), jnp.float32),
-            pltpu.VMEM((s_heads, images, pad, QROWS), jnp.bfloat16),
-            pltpu.VMEM((max(n_tensor - 1, 1), s_here, images, pad, QROWS), jnp.bfloat16),
+            pltpu.VMEM((tokens, width), jnp.bfloat16),
+            pltpu.VMEM((n_tensor, s_part, pad, QROWS), jnp.float32),
+            pltpu.VMEM((heads_here, images, pad + QROWS, HD_T), jnp.bfloat16),
+            pltpu.VMEM((n_tensor - 1, heads_here, pad + QROWS, HD_T), jnp.bfloat16),
+            pltpu.VMEM((s_part, pad, QROWS), jnp.bfloat16),
             pltpu.VMEM((s_here, n_dp * images, pad, QROWS), jnp.bfloat16),
+            dma,
             dma,
             dma(one),
             dma(one),
@@ -351,10 +443,14 @@
             dma(one),
             dma(two),
             dma(two),
-            dma((max(n_tensor - 1, 1), s_here)),
-            dma((max(n_tensor - 1, 1), s_here)),
-            dma((n_dp - 1, s_here)),
-            dma((n_dp - 1, s_here)),
+            dma((heads_here, n_tensor - 1)),
+            dma((heads_here, n_tensor - 1)),
+            dma((images, s_here)),
+            dma((images, s_here)),
+            dma((max(n_x - 1, 1), s_here)),
+            dma((max(n_x - 1, 1), s_here)),
+            dma((n_x, s_here)),
+            dma((n_x, s_here)),
         ],
         compiler_params=pltpu.CompilerParams(
             collective_id=0, has_side_effects=True, vmem_limit_bytes=67043328

time: 239 us -> 223 us (0.933)
  Pallas kernels: 180 us -> 166 us
    pallas_call x1, Pallas kernels: 180 us -> 166 us  [teacher_folded(): pl.pallas_call(functools.partial(teacher_kernel, sizes), out_shape=jax.Sh...]
where the time goes in v3:
time: 223 us; the launch traced here: 222 us
  Pallas kernels  166 us (74%)
  local copies, waits for them, and re-layouts  24.5 us (11%)
  waiting for transfers between devices  16.1 us (7%)
  matrix products  6.89 us (3%)
  other arithmetic  5.92 us (3%)
    pallas_call x1, Pallas kernels, teacher_folded(): pl.pallas_call(functools.partial(teacher_kernel, sizes), out_shape=jax.Sh...  166 us
    unnamed x36, local copies, waits for them, and re-layouts  20.6 us
    ppermute x1, waiting for transfers between devices, sum_over_dp(): mine = mine + lax.ppermute(sent, 'dp', around).astype(jnp.float32)  12.7 us
  transfers between devices with their start and end apart: 3, of which 3 were waited for; matrix products, arithmetic and copies ran while one was open for 0% of the time, Pallas kernels for 0%

profile of v3, /device:TPU:0, one launch (start us, length us, event | category | flops | bytes accessed | tf_op | source)
XLA Modules:
  0.0 222.0 jit_solution(5722395075938125918)
XLA Ops:
  0.0 1.6 convert_reduce_fusion
  1.6 1.7 fusion.5
  3.4 0.5 copy.23
  3.9 0.1 fusion.41
  4.0 0.6 copy-done
  4.6 0.5 fusion.8
  5.1 1.0 copy-done.2
  6.1 0.3 fusion.17
  6.4 0.8 copy.27
  7.2 0.8 convolution_convert_fusion.1
  8.0 0.9 copy.25
  9.0 8.8 %copy.71 = bf16[1536,2,1536]{2,0,1:T(8,128)(2,1)} copy(bf16[1536,2,1536]{2,1,0:T(2,128)(2,1)} %param.11) | data formatting | bytes 18874368 | tf_op args[2]
  17.7 8.2 %copy.32.x_ref = bf16[2,257,6144]{2,1,0:T(8,128)(2,1)} copy(bf16[2,257,6144]{2,0,1:T(2,128)(2,1)} %param.9) | data formatting | bytes 12632064 | tf_op args[0]
  25.9 0.7 copy.31.counts_ref
  26.6 166.1 %shard_map.91 = bf16[4,2,272,128]{3,2,1,0:T(8,128)(2,1)} custom-call(s32[48,16]{1,0:T(8,128)} %copy.31.counts_ref, s32[2]{0:T(128)} %slots_ref.1, bf16[2,257,6144]{2,1,0:T(8,128)(2,1)} %copy.32.x_ref, f32[1,6144]{1,0:T(1,128)} %bitcast.73, bf16[2,1536,1536]{2,1,0:T(8,128)(2,1)} %bitcast.62), custom_call_target="tpu_custom_call" | custom-call | tf_op jit(solution)/shard_map/pallas_call | solution.py:414
  192.8 1.2 fusion
  194.0 2.1 fusion.15
  196.1 0.8 copy-done.15
  196.9 1.6 convolution_bitcast_fusion
  198.6 2.0 convolution_bitcast_fusion.1
  200.6 0.2 pad_maximum_fusion
  200.9 0.2 copy.37
  201.1 0.1 dynamic-slice_convert_fusion
  201.2 0.4 collective-permute-start
  201.6 1.5 collective-permute-done
  203.2 0.2 fusion.21
  203.4 1.6 collective-permute-start.1
  204.9 12.7 %collective-permute-done.1 = bf16[512,512]{0,1:T(8,128)(2,1)S(1)} collective-permute-done((bf16[512,512]{0,1:T(8,128)(2,1)S(1)}, bf16[512,512]{0,1:T(8,128)(2,1)S(1)}, u32[]{:S(2)}, u32[]{:S(2)}) %collective-permute-start.1) | collective-permute-done | bytes 524320 | tf_op jit(solution)/shard_map/ppermute | solution.py:472
  217.6 0.2 add_convert_fusion
  217.9 1.9 collective-permute-done.2
  219.9 0.3 maximum_convert_fusion
  220.1 1.8 copy.38
  (33 shorter events, 0.2 us)
Async XLA Ops:
  0.0 3.3 %copy-start.3 = (bf16[1024,512]{1,0:T(8,128)(2,1)S(1)}, bf16[1024,512]{1,0:T(8,128)(2,1)}, u32[]{:S(2)}) copy-start(bf16[1024,512]{1,0:T(8,128)(2,1)} %param.17) | copy-start | bytes 3145732
  1.6 5.6 %copy-start.6 = (f32[2,257]{1,0:T(2,128)}, f32[2,257]{1,0:T(2,128)S(1)}, u32[]{:S(2)}) copy-start(f32[2,257]{1,0:T(2,128)S(1)} %broadcast_multiply_fusion) | copy-start | bytes 6172
  3.4 3.8 %copy-start.8 = (f32[2,257]{1,0:T(2,128)}, f32[2,257]{1,0:T(2,128)S(1)}, u32[]{:S(2)}) copy-start(f32[2,257]{1,0:T(2,128)S(1)} %add_rsqrt_fusion) | copy-start | bytes 6172
  3.4 1.2 copy-start
  3.4 1.2 copy-start.11
  3.4 1.2 copy-start.13
  5.1 1.0 copy-start.2
  17.7 8.2 %copy-start.10 = (s32[48,16]{0,1:T(8,128)S(1)}, s32[48,16]{0,1:T(8,128)}, u32[]{:S(2)}) copy-start(s32[48,16]{0,1:T(8,128)} %param.12) | copy-start | bytes 9220
  193.9 2.9 %copy-start.4 = (bf16[2,257,256]{1,2,0:T(8,128)(2,1)S(1)}, bf16[2,257,256]{1,2,0:T(8,128)(2,1)}, u32[]{:S(2)}) copy-start(bf16[2,257,256]{1,2,0:T(8,128)(2,1)} %copy.25) | copy-start | bytes 789508
  196.0 0.8 copy-start.15
  196.8 1.7 copy-start.1
  196.9 1.7 copy-start.5
  196.9 1.7 copy-start.7
  196.9 1.7 copy-start.9
  196.9 1.7 copy-start.12
  196.9 1.7 copy-start.14
  201.2 2.0 collective-permute-start
  203.4 14.3 %collective-permute-start.1 = (bf16[512,512]{0,1:T(8,128)(2,1)S(1)}, bf16[512,512]{0,1:T(8,128)(2,1)S(1)}, u32[]{:S(2)}, u32[]{:S(2)}) collective-permute-start(bf16[512,512]{0,1:T(8,128)(2,1)S(1)} %fusion.21), channel_id=1, source_target_pairs={{0,2},{1,3},{2,0},{3,1},{4,6},{5,7},{6,4},{7,5},{8,10},{9,11},{10,... | collective-permute-start | bytes 1572872 | tf_op jit(solution)/shard_map/ppermute | solution.py:472
  217.8 2.0 collective-permute-start.2

commit v4 on v3

--- a/solution.py
+++ b/solution.py
@@ -258,7 +258,7 @@
                     copy_y(k, s, g).start()
                 copy_mate_x(k, s).start()
 
-        @pl.when(k > 0)
+        @pl.when((k > 0) & (k <= heads_here))
         def _():
             j = k - 1
             for s in range(1, n_x):
@@ -285,11 +285,11 @@
             return inner
 
         lax.fori_loop(
-            jnp.where(k <= images, 0, k - 1), jnp.where(k < images, 0, k), ready, 0
+            jnp.where(k <= images, 0, k - 2), jnp.where(k < images, 0, k - 1), ready, 0
         )
         return carry
 
-    lax.fori_loop(0, heads_here + 1, step, 0)
+    lax.fori_loop(0, heads_here + 2, step, 0)
 
     attend(heads_here - 1)
 

time: 223 us -> 219 us (0.982)
  Pallas kernels: 166 us -> 162 us
    pallas_call x1, Pallas kernels: 166 us -> 162 us  [teacher_folded(): pl.pallas_call(functools.partial(teacher_kernel, sizes), out_shape=jax.Sh...]
where the time goes in v4:
time: 219 us; the launch traced here: 218 us
  Pallas kernels  162 us (74%)
  local copies, waits for them, and re-layouts  24.5 us (11%)
  waiting for transfers between devices  16.9 us (8%)
  matrix products  6.89 us (3%)
  other arithmetic  5.92 us (3%)
    pallas_call x1, Pallas kernels, teacher_folded(): pl.pallas_call(functools.partial(teacher_kernel, sizes), out_shape=jax.Sh...  162 us
    unnamed x36, local copies, waits for them, and re-layouts  20.6 us
    ppermute x1, waiting for transfers between devices, sum_over_dp(): mine = mine + lax.ppermute(sent, 'dp', around).astype(jnp.float32)  13.5 us
  transfers between devices with their start and end apart: 3, of which 3 were waited for; matrix products, arithmetic and copies ran while one was open for 0% of the time, Pallas kernels for 0%

profile of v4, /device:TPU:0, one launch (start us, length us, event | category | flops | bytes accessed | tf_op | source)
XLA Modules:
  0.0 218.0 jit_solution(12887227616635636776)
XLA Ops:
  0.0 1.6 convert_reduce_fusion
  1.6 1.7 fusion.5
  3.4 0.5 copy.23
  3.9 0.1 fusion.41
  4.0 0.6 copy-done
  4.6 0.5 fusion.8
  5.1 1.0 copy-done.2
  6.1 0.3 fusion.17
  6.4 0.8 copy.27
  7.2 0.8 convolution_convert_fusion.1
  8.0 0.9 copy.25
  9.0 8.8 %copy.71 = bf16[1536,2,1536]{2,0,1:T(8,128)(2,1)} copy(bf16[1536,2,1536]{2,1,0:T(2,128)(2,1)} %param.11) | data formatting | bytes 18874368 | tf_op args[2]
  17.7 8.2 %copy.32.x_ref = bf16[2,257,6144]{2,1,0:T(8,128)(2,1)} copy(bf16[2,257,6144]{2,0,1:T(2,128)(2,1)} %param.9) | data formatting | bytes 12632064 | tf_op args[0]
  25.9 0.7 copy.31.counts_ref
  26.6 162.2 %shard_map.91 = bf16[4,2,272,128]{3,2,1,0:T(8,128)(2,1)} custom-call(s32[48,16]{1,0:T(8,128)} %copy.31.counts_ref, s32[2]{0:T(128)} %slots_ref.1, bf16[2,257,6144]{2,1,0:T(8,128)(2,1)} %copy.32.x_ref, f32[1,6144]{1,0:T(1,128)} %bitcast.73, bf16[2,1536,1536]{2,1,0:T(8,128)(2,1)} %bitcast.62), custom_call_target="tpu_custom_call" | custom-call | tf_op jit(solution)/shard_map/pallas_call | solution.py:414
  188.8 1.2 fusion
  190.0 2.1 fusion.15
  192.1 0.8 copy-done.15
  192.9 1.6 convolution_bitcast_fusion
  194.6 2.0 convolution_bitcast_fusion.1
  196.7 0.2 pad_maximum_fusion
  196.9 0.2 copy.37
  197.2 0.1 dynamic-slice_convert_fusion
  197.3 0.4 collective-permute-start
  197.7 1.5 collective-permute-done
  199.2 0.2 fusion.21
  199.4 0.8 collective-permute-start.1
  200.2 13.5 %collective-permute-done.1 = bf16[512,512]{0,1:T(8,128)(2,1)S(1)} collective-permute-done((bf16[512,512]{0,1:T(8,128)(2,1)S(1)}, bf16[512,512]{0,1:T(8,128)(2,1)S(1)}, u32[]{:S(2)}, u32[]{:S(2)}) %collective-permute-start.1) | collective-permute-done | bytes 524320 | tf_op jit(solution)/shard_map/ppermute | solution.py:472
  213.7 0.2 add_convert_fusion
  214.0 1.9 collective-permute-done.2
  215.9 0.3 maximum_convert_fusion
  216.2 1.8 copy.38
  (33 shorter events, 0.2 us)
Async XLA Ops:
  0.0 3.3 %copy-start.3 = (bf16[1024,512]{1,0:T(8,128)(2,1)S(1)}, bf16[1024,512]{1,0:T(8,128)(2,1)}, u32[]{:S(2)}) copy-start(bf16[1024,512]{1,0:T(8,128)(2,1)} %param.17) | copy-start | bytes 3145732
  1.6 5.6 %copy-start.6 = (f32[2,257]{1,0:T(2,128)}, f32[2,257]{1,0:T(2,128)S(1)}, u32[]{:S(2)}) copy-start(f32[2,257]{1,0:T(2,128)S(1)} %broadcast_multiply_fusion) | copy-start | bytes 6172
  3.4 3.8 %copy-start.8 = (f32[2,257]{1,0:T(2,128)}, f32[2,257]{1,0:T(2,128)S(1)}, u32[]{:S(2)}) copy-start(f32[2,257]{1,0:T(2,128)S(1)} %add_rsqrt_fusion) | copy-start | bytes 6172
  3.4 1.2 copy-start
  3.4 1.2 copy-start.11
  3.4 1.2 copy-start.13
  5.1 1.0 copy-start.2
  17.7 8.2 %copy-start.10 = (s32[48,16]{0,1:T(8,128)S(1)}, s32[48,16]{0,1:T(8,128)}, u32[]{:S(2)}) copy-start(s32[48,16]{0,1:T(8,128)} %param.12) | copy-start | bytes 9220
  190.0 2.9 %copy-start.4 = (bf16[2,257,256]{1,2,0:T(8,128)(2,1)S(1)}, bf16[2,257,256]{1,2,0:T(8,128)(2,1)}, u32[]{:S(2)}) copy-start(bf16[2,257,256]{1,2,0:T(8,128)(2,1)} %copy.25) | copy-start | bytes 789508
  192.1 0.8 copy-start.15
  192.9 1.7 copy-start.1
  192.9 1.7 copy-start.5
  192.9 1.7 copy-start.7
  192.9 1.7 copy-start.9
  192.9 1.7 copy-start.12
  192.9 1.7 copy-start.14
  197.3 2.0 collective-permute-start
  199.4 14.3 %collective-permute-start.1 = (bf16[512,512]{0,1:T(8,128)(2,1)S(1)}, bf16[512,512]{0,1:T(8,128)(2,1)S(1)}, u32[]{:S(2)}, u32[]{:S(2)}) collective-permute-start(bf16[512,512]{0,1:T(8,128)(2,1)S(1)} %fusion.21), channel_id=1, source_target_pairs={{0,2},{1,3},{2,0},{3,1},{4,6},{5,7},{6,4},{7,5},{8,10},{9,11},{10,... | collective-permute-start | bytes 1572872 | tf_op jit(solution)/shard_map/ppermute | solution.py:472
  213.9 2.0 collective-permute-start.2
